TPU v7x, 512 devices: a whole 4x8x8 slice. The times are simulated.
512 devices in a mesh: batch: 16 (over y, x_lo), centre: 32 (over z, x_hi, core).
Axes of the slice: x: 4 (x_hi: 2, x_lo: 2; x = x_hi * 2 + x_lo), y: 8, z: 8, core: 2. Of those that a mesh axis runs over, the one named last changes fastest.
Arguments:
- batch_pool: bfloat16 [20992, 1024], P(('batch', 'centre')), may hold values from -6 to 6
- batch_index: int32 [16384], P(('batch', 'centre')), may hold values from 0 to 20991, as said below
- centre_pool: bfloat16 [73760, 1024], P('centre'), may hold values from -6 to 6
- centre_index: int32 [65536], P('centre'), may hold values from 0 to 73759, as said below
- targets: float32 [16384, 301], P(('batch', 'centre')), may hold values from -6 to 6
- coefficients: float32 [65536, 301], P('centre'), may hold values from -1.5 to 1.5
Outputs:
- updated: float32 [65536, 301], P('centre')
- residual: float32 [16384, 301], P(('batch', 'centre'))
Inputs may be any that keep to these rules, and one draw needn't show every extreme that they name: `batch_index`: the entries of each aligned block of 32 are distinct and lie in the same aligned block of 41 pool rows, block for block. `centre_index`: the entries of each aligned block of 2048 are distinct and lie in the same aligned block of 2305 pool rows, block for block.
All inputs are finite; a program needn't handle non-finite values.
Results may differ from a plain program's by a relative error of at most 0.0034.
Values may be sent and summed in bfloat16 or wider, within the bound.
A program may use at most 64 MiB of HBM per device.

v0:
```python
import math

import jax
import jax.numpy as jnp
from jax import lax
from jax.sharding import Mesh
from jax.sharding import PartitionSpec as P

CENTRE = ("centre_0", "centre_1", "centre_2")
BATCH_CENTRE = ("batch", "centre_0", "centre_1", "centre_2")


def sent_to_all(value, axis):
    devices = lax.axis_size(axis)
    return lax.all_to_all(
        jnp.broadcast_to(value[None], (devices, *value.shape)), axis, 0, 0, tiled=True
    )


def joined_along(tiles, dim):
    tiles = jnp.moveaxis(tiles, 0, dim)
    dims = tiles.shape
    return tiles.reshape(*dims[:dim], dims[dim] * dims[dim + 1], *dims[dim + 2 :])


def gather_axes(value, axes, dim):
    far, near = axes
    tiles = sent_to_all(sent_to_all(value, far), near)
    return joined_along(tiles.swapaxes(0, 1).reshape(-1, *value.shape), dim)


def in_blocks(value, dim, devices):
    before, after = (value.shape[:dim], value.shape[dim + 1 :])
    return jnp.moveaxis(value.reshape(*before, devices, -1, *after), dim, 0)


def summed_on_arrival(value, axis, dim):
    devices = lax.axis_size(axis)
    tiles = lax.all_to_all(in_blocks(value, dim, devices), axis, 0, 0, tiled=True)
    return jnp.sum(tiles, axis=0)


def summed_rows(value, axes, dim):
    far, near = axes
    own = summed_on_arrival(in_blocks(value, dim, lax.axis_size(far)), near, dim + 1)
    return jnp.sum(lax.all_to_all(own, far, 0, 0, tiled=True), axis=0)


def rows_for(lines, devices):
    spare = -len(lines) % devices
    return jnp.pad(lines, [(0, spare)] + [(0, 0)] * (lines.ndim - 1))


def sum_by_parts(value, axes):
    lines = value.reshape(-1, value.shape[-1])
    own = summed_rows(rows_for(lines, lax.axis_size(axes[0]) * lax.axis_size(axes[1])), axes, 0)
    whole = gather_axes(own, axes, 0)
    return whole[: len(lines)].reshape(value.shape)


def gathered_copies(value, axis, dim):
    tiles = sent_to_all(value, axis)
    return joined_along(tiles, dim)


def nested_sum(value, axes):
    lines = value.reshape(-1, value.shape[-1])
    padded = rows_for(lines, lax.axis_size(axes))
    whole = gathered_copies(summed_on_arrival(padded, axes, 0), axes, 0)
    return lax.slice_in_dim(whole, 0, len(lines)).reshape(value.shape)


def contract_first(left, right):
    return lax.dot_general(
        left, right, (((0,), (0,)), ((), ())), preferred_element_type=jnp.float32
    )


def on_device(batch_pool, batch_index, centre_pool, centre_index, targets, coefficients):
    own_count = batch_index.shape[0]
    device_place = lax.axis_index("batch") * lax.axis_size(CENTRE) + lax.axis_index(CENTRE)
    local_rows = jnp.take(batch_pool, batch_index - device_place * batch_pool.shape[0], axis=0)
    centres = jnp.take(
        centre_pool, centre_index - lax.axis_index(CENTRE) * centre_pool.shape[0], axis=0
    )
    centre_square = jnp.sum(jnp.square(centres.astype(jnp.float32)), axis=1)
    coefficient_half = coefficients.astype(jnp.bfloat16)
    piece = gather_axes(local_rows, (("centre_0", "centre_1"), "centre_2"), 0)
    cross = lax.dot_general(
        piece, centres, (((1,), (1,)), ((), ())), preferred_element_type=jnp.float32
    )
    piece_square = jnp.sum(jnp.square(piece.astype(jnp.float32)), axis=1)
    squared = piece_square[:, None] + centre_square[None, :] - 2.0 * cross
    kernel = jnp.exp(-jnp.sqrt(jnp.maximum(squared, 0.0))).astype(jnp.bfloat16)
    terms = jnp.dot(kernel, coefficient_half, preferred_element_type=jnp.float32)
    row_start = lax.axis_index(CENTRE) * own_count
    placed = lax.dynamic_update_slice_in_dim(jnp.zeros_like(terms), targets, row_start, 0)
    summed = sum_by_parts(terms - placed, (("centre_0", "centre_1"), "centre_2"))
    residual = lax.dynamic_slice_in_dim(summed, row_start, own_count, 0)
    all_half = summed.astype(jnp.bfloat16)
    partial_value = contract_first(kernel, all_half)
    batch_total = own_count * lax.axis_size("batch") * lax.axis_size(CENTRE)
    step_size = 8.0 / math.sqrt(batch_total)
    gradient = nested_sum(partial_value, "batch")
    updated = coefficients - step_size * gradient
    return (updated, residual)


def solution(mesh):
    finer = Mesh(
        mesh.devices.reshape(mesh.shape["batch"], 8, 2, 2),
        ("batch", "centre_0", "centre_1", "centre_2"),
    )
    placed = (
        P(BATCH_CENTRE, None),
        P(BATCH_CENTRE),
        P(CENTRE, None),
        P(CENTRE),
        P(BATCH_CENTRE, None),
        P(CENTRE, None),
    )
    return jax.shard_map(
        on_device,
        mesh=finer,
        in_specs=placed,
        out_specs=(P(CENTRE, None), P(BATCH_CENTRE, None)),
        check_vma=False,
    )
```

profile of v0, /device:TPU:16, one launch (start us, length us, event | category | flops | bytes accessed | tf_op | source)
XLA Modules:
  0.0 275.6 jit_solution(6626914836227450153)
XLA Ops:
  2.2 1.1 broadcast_in_dim.62
  3.3 12.9 %all-to-all-start = ((bf16[16,32,1024]{2,1,0:T(8,128)(2,1)}), bf16[16,32,1024]{2,1,0:T(8,128)(2,1)S(1)}, u32[]{:S(2)}, u32[]{:S(2)}) async-start(bf16[16,32,1024]{2,1,0:T(8,128)(2,1)} %broadcast_in_dim.62), calls=%async_computation | async-start | bytes 2097152 | tf_op jit(solution)/shard_map/all_to_all | solution.py:15
  17.2 13.9 %gather_fusion.1 = bf16[2048,1024]{1,0:T(8,128)(2,1)} fusion(bf16[2305,1024]{1,0:T(8,128)(2,1)} %param.8, s32[2048]{0:T(1024)S(1)} %fusion.10), kind=kCustom, calls=%fused_computation.1 | custom fusion | bytes 8396800 | tf_op jit(solution)/shard_map/jit(_take)/gather | solution.py:83
  31.2 1.3 dynamic_update_slice.3
  32.6 3.5 %multiply_reduce_fusion = f32[2048]{0:T(1024)S(1)} fusion(bf16[2048,1024]{1,0:T(8,128)(2,1)} %gather_fusion.1, pred[2048]{0:T(1024)(128)(4,1)S(1)} %compare_and_fusion), kind=kLoop, calls=%fused_computation.9 | loop fusion | flops 8386560 | bytes 4204544 | tf_op jit(solution)/shard_map/reduce_sum | solution.py:86
  36.1 10.4 %all-to-all-done = bf16[16,32,1024]{2,1,0:T(8,128)(2,1)S(1)} async-done(((bf16[16,32,1024]{2,1,0:T(8,128)(2,1)}), bf16[16,32,1024]{2,1,0:T(8,128)(2,1)S(1)}, u32[]{:S(2)}, u32[]{:S(2)}) %all-to-all-start) | async-done | bytes 1048608 | tf_op jit(solution)/shard_map/all_to_all | solution.py:15
  46.7 5.4 %all_to_all.40 = bf16[2,16,32,1024]{3,2,1,0:T(8,128)(2,1)S(1)} all-to-all(bf16[2,16,32,1024]{3,2,1,0:T(8,128)(2,1)S(1)} %broadcast_in_dim.63), channel_id=1, replica_groups=mesh['batch'=16,'centre_0'=8,'centre_1'=2,'centre_2'=2] {'centre_2'}, dimensions={0} | all-to-all | bytes 4194304 | tf_op jit(solution)/shard_map/all_to_all | solution.py:15
  52.9 2.0 copy-done.2
  54.9 8.6 %fusion.4 = (bf16[2048,1024]{0,1:T(8,128)(2,1)}, f32[1024,2048]{1,0:T(8,128)S(1)}) fusion(f32[2048]{0:T(1024)S(1)} %multiply_reduce_fusion, f32[1024]{0:T(1024)S(1)} %add.60, bf16[1024,1024]{1,0:T(8,128)(2,1)S(1)} %bitcast.40, bf16[2048,1024]{1,0:T(8,128)(2,1)S(1)} %copy-done.2, pred[2048]{0:T(1024)(128)(4,1)S(1)} %compare_and_fusion), kind=kOutput, calls=%fused_computation.7 | convolution fusion | flops 4309647360 | bytes 18888704 | tf_op jit(solution)/shard_map/dot_general | solution.py:89
  63.5 4.3 %fusion.8 = f32[1024,301]{0,1:T(8,128)S(1)} fusion(f32[1024,301]{0,1:T(8,128)S(1)} %copy-done.7, f32[1024,2048]{1,0:T(8,128)S(1)} %get-tuple-element.5, f32[2048]{0:T(1024)S(1)} %multiply_reduce_fusion, f32[1024]{0:T(1024)S(1)} %add.60, f32[2048,301]{0,1:T(8,128)S(1)} %copy-done.4), kind=kOutput, calls=%fused_computation.16 | convolution fusion | flops 1275993088 | bytes 13332480 | tf_op jit(solution)/shard_map/dot_general | solution.py:95
  68.5 5.0 %all_to_all.41 = f32[2,16,32,301]{3,2,1,0:T(8,128)S(1)} all-to-all(f32[2,16,32,301]{3,2,1,0:T(8,128)S(1)} %copy.43), channel_id=1, replica_groups=mesh['batch'=16,'centre_0'=8,'centre_1'=2,'centre_2'=2] {'centre_2'}, dimensions={0} | all-to-all | bytes 2465792 | tf_op jit(solution)/shard_map/all_to_all | solution.py:39
  73.6 28.4 %all_to_all.42 = f32[16,32,301]{2,1,0:T(8,128)S(1)} all-to-all(f32[16,32,301]{2,1,0:T(8,128)S(1)} %reduce_sum.47), channel_id=1, replica_groups=mesh['batch'=16,'centre_0'=8,'centre_1'=2,'centre_2'=2] {'centre_0','cen..., dimensions={0} | all-to-all | bytes 1232896 | tf_op jit(solution)/shard_map/all_to_all | solution.py:46
  103.1 3.6 %all-to-all-start.4 = ((f32[16,32,301]{2,1,0:T(8,128)}), f32[16,32,301]{2,1,0:T(8,128)S(1)}, u32[]{:S(2)}, u32[]{:S(2)}) async-start(f32[16,32,301]{2,1,0:T(8,128)} %broadcast_in_dim.68), calls=%async_computation.4 | async-start | bytes 1572864 | tf_op jit(solution)/shard_map/all_to_all | solution.py:15
  106.7 6.4 %copy.50 = bf16[2048,1024]{1,0:T(8,128)(2,1)} copy(bf16[2048,1024]{0,1:T(8,128)(2,1)} %get-tuple-element.4) | data formatting | bytes 8388608 | tf_op jit(solution)/shard_map/dot_general | solution.py:74
  113.1 17.2 %all-to-all-done.4 = f32[16,32,301]{2,1,0:T(8,128)S(1)} async-done(((f32[16,32,301]{2,1,0:T(8,128)}), f32[16,32,301]{2,1,0:T(8,128)S(1)}, u32[]{:S(2)}, u32[]{:S(2)}) %all-to-all-start.4) | async-done | bytes 616480 | tf_op jit(solution)/shard_map/all_to_all | solution.py:15
  130.5 5.3 %all_to_all.43 = f32[2,16,32,301]{3,2,1,0:T(8,128)S(1)} all-to-all(f32[2,16,32,301]{3,2,1,0:T(8,128)S(1)} %broadcast_in_dim.69), channel_id=1, replica_groups=mesh['batch'=16,'centre_0'=8,'centre_1'=2,'centre_2'=2] {'centre_2'}, dimensions={0} | all-to-all | bytes 2465792 | tf_op jit(solution)/shard_map/all_to_all | solution.py:15
  136.0 1.5 fusion.14
  137.5 65.3 %all_to_all.44 = f32[16,128,301]{1,2,0:T(8,128)} all-to-all(f32[16,128,301]{1,2,0:T(8,128)S(1)} %fusion.14), channel_id=1, replica_groups=mesh['batch'=16,'centre_0'=8,'centre_1'=2,'centre_2'=2] {'batch'}, dimensions={0} | all-to-all | bytes 4931584 | tf_op jit(solution)/shard_map/all_to_all | solution.py:39
  202.7 1.8 reduce_sum.49
  204.6 1.6 broadcast_in_dim.70
  206.2 6.3 %all-to-all-start.7 = ((f32[16,128,301]{1,2,0:T(8,128)}), f32[16,128,301]{1,2,0:T(8,128)}, u32[]{:S(2)}, u32[]{:S(2)}) async-start(f32[16,128,301]{1,2,0:T(8,128)} %broadcast_in_dim.70), calls=%async_computation.7 | async-start | bytes 4980736 | tf_op jit(solution)/shard_map/all_to_all | solution.py:15
  213.3 56.2 %all-to-all-done.7 = f32[16,128,301]{1,2,0:T(8,128)} async-done(((f32[16,128,301]{1,2,0:T(8,128)}), f32[16,128,301]{1,2,0:T(8,128)}, u32[]{:S(2)}, u32[]{:S(2)}) %all-to-all-start.7) | async-done | bytes 2465824 | tf_op jit(solution)/shard_map/all_to_all | solution.py:15
  269.5 2.6 fusion.6
  273.8 1.8 sub.31
  (41 shorter events, 8.3 us)
Async XLA Ops:
  0.6 0.9 copy-start
  0.6 16.5 %copy-start.8 = (s32[2048]{0:T(1024)S(1)}, s32[2048]{0:T(1024)}, u32[]{:S(2)}) copy-start(s32[2048]{0:T(1024)} %param.9) | copy-start | bytes 24580
  3.3 43.1 %all-to-all-start = ((bf16[16,32,1024]{2,1,0:T(8,128)(2,1)}), bf16[16,32,1024]{2,1,0:T(8,128)(2,1)S(1)}, u32[]{:S(2)}, u32[]{:S(2)}) async-start(bf16[16,32,1024]{2,1,0:T(8,128)(2,1)} %broadcast_in_dim.62), calls=%async_computation | async-start | bytes 2097152 | tf_op jit(solution)/shard_map/all_to_all | solution.py:15
  32.5 14.0 %copy-start.6 = (f32[1024,301]{0,1:T(8,128)}, f32[1024,301]{0,1:T(8,128)S(1)}, u32[]{:S(2)}) copy-start(f32[1024,301]{0,1:T(8,128)S(1)} %dynamic_update_slice.3) | copy-start | bytes 3698692
  52.7 2.2 copy-start.2
  54.9 8.6 %copy-start.4 = (f32[2048,301]{0,1:T(8,128)S(1)}, f32[2048,301]{0,1:T(8,128)}, u32[]{:S(2)}) copy-start(f32[2048,301]{0,1:T(8,128)} %param.11) | copy-start | bytes 7397380
  54.9 8.6 %copy-start.7 = (f32[1024,301]{0,1:T(8,128)S(1)}, f32[1024,301]{0,1:T(8,128)}, u32[]{:S(2)}) copy-start(f32[1024,301]{0,1:T(8,128)} %copy-done.6) | copy-start | bytes 3698692
  103.1 27.2 %all-to-all-start.4 = ((f32[16,32,301]{2,1,0:T(8,128)}), f32[16,32,301]{2,1,0:T(8,128)S(1)}, u32[]{:S(2)}, u32[]{:S(2)}) async-start(f32[16,32,301]{2,1,0:T(8,128)} %broadcast_in_dim.68), calls=%async_computation.4 | async-start | bytes 1572864 | tf_op jit(solution)/shard_map/all_to_all | solution.py:15
  130.3 5.7 %copy-start.3 = (bf16[2048,1024]{1,0:T(8,128)(2,1)S(1)}, bf16[2048,1024]{1,0:T(8,128)(2,1)}, u32[]{:S(2)}) copy-start(bf16[2048,1024]{1,0:T(8,128)(2,1)} %copy.50) | copy-start | bytes 12582916
  206.2 63.3 %all-to-all-start.7 = ((f32[16,128,301]{1,2,0:T(8,128)}), f32[16,128,301]{1,2,0:T(8,128)}, u32[]{:S(2)}, u32[]{:S(2)}) async-start(f32[16,128,301]{1,2,0:T(8,128)} %broadcast_in_dim.70), calls=%async_computation.7 | async-start | bytes 4980736 | tf_op jit(solution)/shard_map/all_to_all | solution.py:15
  272.1 1.7 copy-start.5
  272.3 3.4 %copy-start.1 = (bf16[41,1024]{1,0:T(8,128)(2,1)S(1)}, bf16[41,1024]{1,0:T(8,128)(2,1)}, u32[]{:S(2)}) copy-start(bf16[41,1024]{1,0:T(8,128)(2,1)} %param.6) | copy-start | bytes 251908
where the time goes:
time: 276 us
  blocking collectives  109 us (39%)
  waiting for transfers between devices  83.8 us (30%)
  local copies, waits for them, and re-layouts  33 us (12%)
  starting transfers between devices  22.8 us (8%)
  matrix products  14.4 us (5%)
  other arithmetic  11.4 us (4%)
    all_to_all x3, waiting for transfers between devices, sent_to_all(): lax.all_to_all(jnp.broadcast_to(value[None], (devices, *value.shape)), ax...  83.8 us
    all_to_all x2, blocking collectives, summed_on_arrival(): lax.all_to_all(in_blocks(value, dim, devices), axis, 0, 0, tiled=True)  70.2 us
    all_to_all x1, blocking collectives, summed_rows(): return jnp.sum(lax.all_to_all(own, far, 0, 0, tiled=True), axis=0)  28.4 us
    all_to_all x3, starting transfers between devices, sent_to_all(): lax.all_to_all(jnp.broadcast_to(value[None], (devices, *value.shape)), ax...  22.8 us
    gather x1, local copies, waits for them, and re-layouts, on_device(): jnp.take(centre_pool, centre_index - lax.axis_index(CENTRE) * centre_pool...  13.9 us
    all_to_all x2, blocking collectives, sent_to_all(): lax.all_to_all(jnp.broadcast_to(value[None], (devices, *value.shape)), ax...  10.7 us
    dot_general x1, matrix products, on_device(): lax.dot_general(piece, centres, (((1,), (1,)), ((), ())), preferred_eleme...  8.59 us
    dot_general x1, local copies, waits for them, and re-layouts, contract_first(): lax.dot_general(left, right, (((0,), (0,)), ((), ())), preferred_element_...  6.43 us
  transfers between devices with their start and end apart: 3, of which 3 were waited for; matrix products, arithmetic and copies ran while one was open for 10% of the time, Pallas kernels for 0%

commit v1 on v0

v1 whole, which is shorter than its diff:
```python
import functools
import math

import jax
import jax.numpy as jnp
from jax import lax
from jax.experimental import pallas as pl
from jax.experimental.pallas import tpu as pltpu
from jax.sharding import PartitionSpec as P

MESH = pl.DeviceIdType.MESH
F32 = jnp.float32
BF16 = jnp.bfloat16
RING = 8
NT = (((1,), (1,)), ((), ()))
NN = (((1,), (0,)), ((), ()))
TN = (((0,), (0,)), ((), ()))
PLACE = (0, 2, 4, 6, 1, 7, 5, 3)
COPIES = 128


def up(n, k):
    return -(-n // k) * k


def dot(a, b, dims):
    return lax.dot_general(a, b, dims, preferred_element_type=F32)


def step_kernel(
    zs, ys, bidx, bpool, cidx, cpool, tgt, coef, grad_out, res_out,
    bsel, xall, pool, tailp, cs, oht, coefv, coefb, coefp, kt, predv, psend, precv,
    qsend, qrecv, tg, tt, res, rq, rt, gp, gpb, ysend, yrecv, fin, xsend, xrecv, grad,
    ssem, rsem, lsem, osem,
):
    bi = lax.axis_index("batch")
    ci = lax.axis_index("centre")
    y, xl = bi // 2, bi % 2
    z, x, c = ci // 4, (ci // 2) % 2, ci % 2
    rows, d = tgt.shape[0], bpool.shape[1]
    out = tgt.shape[1]
    cen = cidx.shape[1]
    n_pool = cpool.shape[0]
    pp = kt.shape[0]
    pm = n_pool // 256 * 256
    lanes = 4 * rows
    half, quart = predv.shape[0] // 2, predv.shape[0] // 4
    og = gp.shape[0]
    cut = up(og // 2, 16)
    chunk = cen // RING
    sub = chunk // 2

    def at(z_, x_, c_):
        return (bi, lax.rem(z_ + 2 * RING, RING) * 4 + x_ * 2 + c_)

    def at_y(y_, xl_):
        return (lax.rem(y_ + 2 * RING, RING) * 2 + xl_, ci)

    count = [0]
    started = []

    def send(src, dst, dev):
        n = count[0]
        count[0] += 1
        copy = pltpu.make_async_remote_copy(
            src_ref=src, dst_ref=dst, send_sem=ssem.at[n], recv_sem=rsem.at[n],
            device_id=dev, device_id_type=MESH,
        )
        copy.start()
        started.append(copy)
        return copy

    partner = at(z, x, 1 - c)
    facing = at(z, 1 - x, c)
    across = at(z, 1 - x, 1 - c)
    greet = []
    if zs:
        greet += [partner, facing, across]
        greet += [at(z + s, x, c) for s in range(1, RING)]
        greet += [at(z + s, 1 - x, c) for s in range(1, RING)]
    if ys:
        greet += [at_y(y + 1, xl), at_y(y - 1, xl), at_y(y, 1 - xl)]
    barrier = pltpu.get_barrier_semaphore()
    for dev in greet:
        pl.semaphore_signal(barrier, inc=1, device_id=dev, device_id_type=MESH)

    load_pool = pltpu.make_async_copy(cpool, pool, lsem.at[0])
    load_pool.start()
    load_coef = pltpu.make_async_copy(coef, coefv, lsem.at[1])
    load_coef.start()

    def rows_at(k):
        return pl.ds(pl.multiple_of(k * rows, rows), rows)

    def quart_at(k):
        return pl.ds(pl.multiple_of(k * quart, 16), quart)

    def half_at(k):
        return pl.ds(pl.multiple_of(k * half, 16), half)

    j = c * 2 + x
    jx = c * 2 + 1 - x

    bsel[...] = jnp.zeros_like(bsel)
    bsel[0 : bpool.shape[0], :] = bpool[...]
    base = (bi * lax.axis_size("centre") + ci) * bpool.shape[0]
    place = lax.broadcasted_iota(jnp.int32, (bsel.shape[0], rows), 0) + base
    pick = jnp.where(place == bidx[...], -2.0, 0.0).astype(BF16)
    xall[0, rows_at(j), :] = dot(pick, bsel[...], TN).astype(BF16)
    tg[rows_at(j), :] = jnp.zeros((rows, tg.shape[1]), F32)
    tg[rows_at(j), 0:out] = tgt[...]

    pl.semaphore_wait(barrier, len(greet))

    ring = {}
    mate = {}
    if zs:
        own = xall.at[0, rows_at(j)]
        cross_x = send(own, own, facing)
        for way, slot in ((1, RING - 1), (-1, 1)):
            ring[way, 1, 0] = send(own, xall.at[PLACE[slot], rows_at(j)], at(z + way, x, c))
        mate[0, 0] = send(own, own, partner)
        mine = tg.at[rows_at(j)]
        tg_sent = [send(mine, mine, dev) for dev in (partner, facing, across)]

    def slot_of(way, level):
        return RING - level if way == 1 else level

    def forward(level):
        if not zs:
            return
        for stream, place_of in ((0, j), (1, jx)):
            for way in (1, -1):
                if level == 0:
                    if way == 1:
                        if stream == 0:
                            continue
                        cross_x.wait_recv()
                        block = xall.at[0, rows_at(jx)]
                        mate[0, 1] = send(block, block, partner)
                    elif stream == 0:
                        continue
                else:
                    if level == 4 and (way == 1) != (stream == 0):
                        continue
                    ring[way, level, stream].wait_recv()
                slot = slot_of(way, level) % RING
                block = xall.at[PLACE[slot], rows_at(place_of)]
                if level < 4 and (level < 3 or (way == 1) == (stream == 0)):
                    nxt = slot_of(way, level + 1)
                    ring[way, level + 1, stream] = send(
                        block, xall.at[PLACE[nxt], rows_at(place_of)], at(z + way, x, c)
                    )
                if level:
                    mate[slot, stream] = send(block, block, partner)

    def ready(slots):
        if zs:
            for s in slots:
                mate[s, 0].wait_recv()
                mate[s, 1].wait_recv()

    cbase = ci * n_pool
    step_rows = 32

    def build(m, carry):
        r0 = pl.multiple_of(m * step_rows, step_rows)
        at_row = lax.broadcasted_iota(jnp.int32, (step_rows, cen), 0) + (cbase + r0)
        oht[pl.ds(r0, step_rows), :] = jnp.where(at_row == cidx[...], 1.0, 0.0).astype(BF16)
        return carry

    lax.fori_loop(0, pp // step_rows, build, 0)
    forward(0)

    load_coef.wait()
    coefb[...] = jnp.zeros_like(coefb)
    coefb[0:out, :] = coefv[...].astype(BF16)
    if og < coefp.shape[0]:
        coefp[og:, :] = jnp.zeros_like(coefp[og:, :])

    def permute(n, width):
        n = pl.multiple_of(n, 128)
        coefp[0:og, pl.ds(n, width)] = dot(
            coefb[...], oht[pl.ds(n, width), :], NT
        ).astype(BF16)

    def permute_body(m, carry):
        permute(m * 256, 256)
        return carry

    lax.fori_loop(0, pm // 256, permute_body, 0)
    permute(pm, pp - pm)
    forward(1)

    load_pool.wait()
    tailp[...] = jnp.zeros_like(tailp)
    tailp[0 : n_pool - pm, :] = pool[pm:n_pool, :]

    def squares(m, carry):
        r0 = pl.multiple_of(m * 128, 128)
        wide = pool[pl.ds(r0, 128), :].astype(F32)
        cs[pl.ds(r0, 128), :] = jnp.broadcast_to(
            jnp.sum(wide * wide, axis=1, keepdims=True), (128, 128)
        )
        return carry

    lax.fori_loop(0, pm // 128, squares, 0)
    wide_tail = tailp[...].astype(F32)
    cs_tail = jnp.sum(wide_tail * wide_tail, axis=1, keepdims=True)
    kt[pm:, :] = jnp.zeros_like(kt[pm:, :])

    def near(squared):
        return jnp.exp(-jnp.sqrt(jnp.maximum(squared, 0.0))).astype(BF16)

    def kernel_of(p0, n):
        width = n * lanes
        cols = slice(p0 * lanes, p0 * lanes + width)
        feats = xall[p0 : p0 + n].reshape(width, d)
        wide = feats.astype(F32)
        square = wide * wide * 0.25
        high = square.astype(BF16)
        low = (square - high.astype(F32)).astype(BF16)
        ones = jnp.ones((16, d), BF16)
        row = (dot(ones, high, NT) + dot(ones, low, NT))[0:1, :]

        def body(m, carry):
            r0 = pl.multiple_of(m * 256, 256)
            both = dot(pool[pl.ds(r0, 256), :], xall[p0 : p0 + n].reshape(width, d), NT)
            col = cs[pl.ds(r0, 256), :]
            col = jnp.concatenate([col] * (width // 128), axis=1) if width > 128 else col[:, :width]
            kt[pl.ds(r0, 256), cols] = near(row + col + both)
            return carry

        lax.fori_loop(0, pm // 256, body, 0)
        both = dot(tailp[...], feats, NT)
        real = lax.broadcasted_iota(jnp.int32, both.shape, 0) < n_pool - pm
        kt[pm : pm + 16, cols] = jnp.where(real, near(row + cs_tail + both), 0.0).astype(BF16)
        predv[:, cols] = dot(coefp[...], kt[:, cols], NN)

    core_sent = {}
    quart_sent = {}

    def lane_of(s):
        return slice(PLACE[s] * lanes, (PLACE[s] + 1) * lanes)

    def share(slots):
        if zs:
            for s in slots:
                psend[PLACE[s]] = predv[half_at(1 - c), lane_of(s)].astype(BF16)
                core_sent[s] = send(psend.at[PLACE[s]], precv.at[PLACE[s]], partner)

    def spread(slots):
        if not zs:
            return
        for s in slots:
            core_sent[s].wait_recv()
            predv[half_at(c), lane_of(s)] += precv[PLACE[s]].astype(F32)
            back = PLACE[(RING - s) % RING]
            for k, xd in ((0, x), (1, 1 - x)):
                if s == 0 and k == 0:
                    continue
                qsend[PLACE[s], k] = predv[quart_at(c * 2 + xd), lane_of(s)].astype(BF16)
                quart_sent[s, k] = send(
                    qsend.at[PLACE[s], k], qrecv.at[back, k], at(z + s, xd, c)
                )

    ready((0,))
    kernel_of(0, 1)
    share((0,))
    forward(2)
    ready((1, 7))
    kernel_of(PLACE[1], 2)
    share((1, 7))
    spread((0,))
    forward(3)
    ready((2, 6))
    kernel_of(PLACE[2], 2)
    share((2, 6))
    spread((1, 7))
    forward(4)
    ready((3, 5))
    kernel_of(PLACE[3], 2)
    share((3, 5))
    spread((2, 6))
    ready((4,))
    kernel_of(1, 1)
    share((4,))
    spread((3, 5))
    if zs:
        for copy in tg_sent:
            copy.wait_recv()
    tt[...] = tg[...].T
    spread((4,))

    total = predv[quart_at(j), lane_of(0)]
    for s in (0, 1, 7, 2, 6, 3, 5, 4):
        for k in (0, 1):
            if (s, k) in quart_sent:
                quart_sent[s, k].wait_recv()
                total = total + qrecv[PLACE[(RING - s) % RING], k].astype(F32)
    mine_now = total - tt[quart_at(j), :]
    res[0, quart_at(j), :] = mine_now.astype(BF16)
    rq[quart_at(j), :] = mine_now
    if zs:
        quarter = res.at[0, quart_at(j)]
        res_x = send(quarter, quarter, facing)
        far = (4, 3, 5, 2, 6, 1, 7)
        res_z = {}
        for s in far:
            res_z[s, 0] = send(
                quarter, res.at[PLACE[(RING - s) % RING], quart_at(j)], at(z + s, x, c)
            )
        res_x.wait_recv()
        other = res.at[0, quart_at(jx)]
        for s in far:
            res_z[s, 1] = send(
                other, res.at[PLACE[(RING - s) % RING], quart_at(jx)], at(z + s, x, c)
            )
        res_mate = {}
        block = res.at[0, half_at(c)]
        res_mate[0] = send(block, block, partner)
        wide_q = rq.at[quart_at(j)]
        rq_sent = [send(wide_q, wide_q, dev) for dev in (partner, facing, across)]
        for s in (1, 7, 2, 6, 3, 5, 4):
            back = (RING - s) % RING
            res_z[back, 0].wait_recv()
            res_z[back, 1].wait_recv()
            block = res.at[PLACE[s], half_at(c)]
            res_mate[s] = send(block, block, partner)

    def res_ready(slots):
        if zs:
            for s in slots:
                res_mate[s].wait_recv()

    def gradient(p0, n, first):
        cols = slice(p0 * lanes, (p0 + n) * lanes)
        left = jnp.concatenate([res[p, 0:og, :] for p in range(p0, p0 + n)], axis=1)

        def part(n0, width):
            n0 = pl.multiple_of(n0, 128)
            term = dot(left, kt[pl.ds(n0, width), cols], NT)
            if first:
                gp[:, pl.ds(n0, width)] = term
            else:
                gpb[:, pl.ds(n0, width)] = (gp[:, pl.ds(n0, width)] + term).astype(BF16)

        def body(m, carry):
            part(m * 256, 256)
            return carry

        lax.fori_loop(0, pm // 256, body, 0)
        part(pm, pp - pm)

    res_ready((1, 7, 2, 6, 3, 5))
    gradient(2, 6, True)
    res_ready((4, 0))
    gradient(0, 2, False)

    def own_term(s, h):
        col = lax.rem(y + s + RING, RING) * chunk + h * sub
        return dot(gpb[...], oht[:, pl.ds(pl.multiple_of(col, 128), sub)], NN)

    if ys:
        chain = {}
        for t in range(1, 5):
            s = 5 - t
            for h in (0, 1):
                terms = {1: own_term(s, h)}
                terms[-1] = terms[1] if t == 1 else own_term(-s, h)
                for w, way in enumerate((1, -1)):
                    first = slice(0, cut) if way == 1 else slice(cut, og)
                    if t == 1:
                        ysend[w, 0, h, first, :] = terms[way][first].astype(BF16)
                        chain[way, t, h] = send(
                            ysend.at[w, 0, h, first], yrecv.at[w, 0, h, first], at_y(y + way, xl)
                        )
                        continue
                    chain[way, t - 1, h].wait_recv()
                    if t == 2:
                        rest = slice(cut, og) if way == 1 else slice(0, cut)
                        ysend[w, 1, h, first, :] = (
                            terms[way][first] + yrecv[w, 0, h, first, :].astype(F32)
                        ).astype(BF16)
                        ysend[w, 1, h, rest, :] = terms[way][rest].astype(BF16)
                    else:
                        ysend[w, t - 1, h] = (
                            terms[way] + yrecv[w, t - 2, h].astype(F32)
                        ).astype(BF16)
                    chain[way, t, h] = send(
                        ysend.at[w, t - 1, h], yrecv.at[w, t - 1, h], at_y(y + way, xl)
                    )
        for h in (0, 1):
            fin[h] = own_term(0, h)
        for h in (0, 1):
            chain[1, 4, h].wait_recv()
            chain[-1, 4, h].wait_recv()
            fin[h] = fin[h] + yrecv[0, 3, h].astype(F32) + yrecv[1, 3, h].astype(F32)
        xsend[...] = fin[1 - xl].astype(BF16)
        swap = send(xsend, xrecv, at_y(y, 1 - xl))
        swap.wait_recv()
        grad[0, xl] = (fin[xl] + xrecv[...].astype(F32)).astype(BF16)
        own = grad.at[0, xl]
        back = {}
        for way, slot in ((1, RING - 1), (-1, 1)):
            back[way, 1, 0] = send(own, grad.at[slot, xl], at_y(y + way, xl))
        cross_l = send(own, own, at_y(y, 1 - xl))
    else:
        for s in range(RING):
            for h in (0, 1):
                grad[s, h] = own_term(s, h).astype(BF16)

    stores = []

    def store(s, h):
        col = lax.rem(y + s, RING) * chunk + h * sub
        copy = pltpu.make_async_copy(
            grad.at[s, h],
            grad_out.at[:, pl.ds(pl.multiple_of(col, 128), sub)],
            osem.at[len(stores)],
        )
        copy.start()
        stores.append(copy)

    if ys:
        store(0, xl)
        cross_l.wait_recv()
        other = grad.at[0, 1 - xl]
        for way, slot in ((1, RING - 1), (-1, 1)):
            back[way, 1, 1] = send(other, grad.at[slot, 1 - xl], at_y(y + way, xl))
        store(0, 1 - xl)
        for level in range(1, 5):
            for stream, h in ((0, xl), (1, 1 - xl)):
                for way in (1, -1):
                    straight = (way == 1) == (stream == 0)
                    if level == 4 and not straight:
                        continue
                    back[way, level, stream].wait_recv()
                    slot = slot_of(way, level)
                    if level < 3 or (level == 3 and straight):
                        back[way, level + 1, stream] = send(
                            grad.at[slot, h], grad.at[slot_of(way, level + 1), h],
                            at_y(y + way, xl),
                        )
                    store(slot, h)
                    if level == 1 and stream == 0 and way == 1 and zs:
                        for copy in rq_sent:
                            copy.wait_recv()
                        rt[...] = rq[...].T
                        res_out[...] = rt[rows_at(j), 0:out]
    else:
        for s in range(RING):
            for h in (0, 1):
                store(s, h)
        if zs:
            for copy in rq_sent:
                copy.wait_recv()
        rt[...] = rq[...].T
        res_out[...] = rt[rows_at(j), 0:out]
    for copy in stores:
        copy.wait()
    for copy in started:
        copy.wait_send()


def on_device(zs, ys, bpool, bidx, cpool, cidx, tgt, coef):
    rows, d = bidx.shape[0], bpool.shape[1]
    out, cen = tgt.shape[1], cidx.shape[0]
    n_pool = cpool.shape[0]
    outp, og = up(out, 64), up(out, 16)
    pp = n_pool // 256 * 256 + 128
    lanes = 4 * rows
    half, quart = outp // 2, outp // 4
    wide = up(outp, 128)
    chunk = cen // RING
    sub = chunk // 2
    vmem = pl.BlockSpec(memory_space=pltpu.VMEM)
    hbm = pl.BlockSpec(memory_space=pl.ANY)
    grad, residual = pl.pallas_call(
        functools.partial(step_kernel, zs, ys),
        out_shape=(
            jax.ShapeDtypeStruct((og, cen), BF16),
            jax.ShapeDtypeStruct((rows, out), F32),
        ),
        in_specs=[vmem, vmem, vmem, hbm, vmem, hbm],
        out_specs=(hbm, vmem),
        scratch_shapes=[
            pltpu.VMEM((up(bpool.shape[0], 16), d), BF16),
            pltpu.VMEM((RING, lanes, d), BF16),
            pltpu.VMEM((n_pool, d), BF16),
            pltpu.VMEM((16, d), BF16),
            pltpu.VMEM((pp, 128), F32),
            pltpu.VMEM((pp, cen), BF16),
            pltpu.VMEM((out, cen), F32),
            pltpu.VMEM((og, cen), BF16),
            pltpu.VMEM((outp, pp), BF16),
            pltpu.VMEM((pp, RING * lanes), BF16),
            pltpu.VMEM((outp, RING * lanes), F32),
            pltpu.VMEM((RING, half, lanes), BF16),
            pltpu.VMEM((RING, half, lanes), BF16),
            pltpu.VMEM((RING, 2, quart, lanes), BF16),
            pltpu.VMEM((RING, 2, quart, lanes), BF16),
            pltpu.VMEM((lanes, wide), F32),
            pltpu.VMEM((wide, lanes), F32),
            pltpu.VMEM((RING, outp, lanes), BF16),
            pltpu.VMEM((outp, lanes), F32),
            pltpu.VMEM((lanes, outp), F32),
            pltpu.VMEM((og, pp), F32),
            pltpu.VMEM((og, pp), BF16),
            pltpu.VMEM((2, 4, 2, og, sub), BF16),
            pltpu.VMEM((2, 4, 2, og, sub), BF16),
            pltpu.VMEM((2, og, sub), F32),
            pltpu.VMEM((og, sub), BF16),
            pltpu.VMEM((og, sub), BF16),
            pltpu.VMEM((RING, 2, og, sub), BF16),
            pltpu.SemaphoreType.DMA((COPIES,)),
            pltpu.SemaphoreType.DMA((COPIES,)),
            pltpu.SemaphoreType.DMA((2,)),
            pltpu.SemaphoreType.DMA((2 * RING,)),
        ],
        compiler_params=pltpu.CompilerParams(
            collective_id=0, has_side_effects=True, vmem_limit_bytes=62 * 1024 * 1024
        ),
        name="regression_step",
    )(
        bidx.reshape(1, rows), bpool, cidx.reshape(1, cen), cpool, tgt, coef.T,
    )
    batch_total = rows * lax.axis_size("batch") * lax.axis_size("centre")
    step_size = 8.0 / math.sqrt(batch_total)
    updated = coef - step_size * grad[:out].astype(F32).T
    return updated, residual


def solution(mesh):
    both = ("batch", "centre")
    zs, ys = mesh.shape["centre"] > 1, mesh.shape["batch"] > 1
    return jax.shard_map(
        functools.partial(on_device, zs, ys),
        mesh=mesh,
        in_specs=(
            P(both, None), P(both), P("centre", None), P("centre"), P(both, None), P("centre", None),
        ),
        out_specs=(P("centre", None), P(both, None)),
        check_vma=False,
    )
```

time: 276 us -> 129 us (0.47)
  the two profiles are of different devices: /device:TPU:16 before, /device:TPU:8 now
where the time goes in v1:
time: 129 us
  Pallas kernels  124 us (96%)
  other arithmetic  3.97 us (3%)
    pallas_call x1, Pallas kernels, on_device(): pl.pallas_call(functools.partial(step_kernel, zs, ys), out_shape=(jax.Sha...  124 us
    sub x1, other arithmetic, on_device(): updated = coef - step_size * grad[:out].astype(F32).T  3.97 us

profile of v1, /device:TPU:8, one launch (start us, length us, event | category | flops | bytes accessed | tf_op | source)
XLA Modules:
  0.0 129.3 jit_solution(14461281572734481524)
XLA Ops:
  0.6 124.1 %regression_step.1 = (bf16[304,2048]{1,0:T(8,128)(2,1)}, f32[32,301]{1,0:T(8,128)}) custom-call(s32[1,32]{1,0:T(1,128)} %bitcast.7, bf16[41,1024]{1,0:T(8,128)(2,1)} %bpool.1, s32[1,2048]{1,0:T(1,128)} %bitcast.6, bf16[2305,1024]{1,0:T(8,128)(2,1)} %cpool.1, f32[32,301]{1,0:T(8,128)} %tgt.1, f32[301,2048]{1,0:T(8,128)} %bitcast.5), custom_call_target="tpu_custom_call" | custom-call | tf_op jit(solution)/shard_map/regression_step/pallas_call | solution.py:479
  124.7 0.0 copy-start
  124.7 4.0 %bitcast_subtract_fusion = f32[2048,301]{0,1:T(8,128)} fusion(f32[2048,301]{0,1:T(8,128)} %param.11, bf16[304,2048]{1,0:T(8,128)(2,1)} %get-tuple-element.4), kind=kLoop, calls=%fused_computation | loop fusion | flops 1849344 | bytes 6164480 | tf_op jit(solution)/shard_map/sub | solution.py:530
  128.7 0.0 copy-done
  128.7 0.6 copy.9
Async XLA Ops:
  124.7 4.0 %copy-start = (f32[32,301]{1,0:T(8,128)S(1)}, f32[32,301]{1,0:T(8,128)}, u32[]{:S(2)}) copy-start(f32[32,301]{1,0:T(8,128)} %get-tuple-element.9) | copy-start | bytes 115588

commit v2 on v1

--- a/solution.py
+++ b/solution.py
@@ -15,8 +15,9 @@
 NT = (((1,), (1,)), ((), ()))
 NN = (((1,), (0,)), ((), ()))
 TN = (((0,), (0,)), ((), ()))
-PLACE = (0, 2, 4, 6, 1, 7, 5, 3)
+PLACE = (0, 1, 3, 5, 7, 6, 4, 2)
 COPIES = 128
+LOG2E = 1.4426950408889634
 
 
 def up(n, k):
@@ -27,9 +28,13 @@
     return lax.dot_general(a, b, dims, preferred_element_type=F32)
 
 
-def step_kernel(
-    zs, ys, bidx, bpool, cidx, cpool, tgt, coef, grad_out, res_out,
-    bsel, xall, pool, tailp, cs, oht, coefv, coefb, coefp, kt, predv, psend, precv,
+def step_kernel(*refs):
+    inner_kernel([], *refs)
+
+
+def inner_kernel(
+    started, zs, ys, bidx, bpool, cidx, cpool, ctail, tgt, coef, grad_out, res_out,
+    bsel, xall, pool, cs, oht, coefv, coefb, coefp, kt, predv, psend, precv,
     qsend, qrecv, tg, tt, res, rq, rt, gp, gpb, ysend, yrecv, fin, xsend, xrecv, grad,
     ssem, rsem, lsem, osem,
 ):
@@ -43,6 +48,8 @@
     n_pool = cpool.shape[0]
     pp = kt.shape[0]
     pm = n_pool // 256 * 256
+    full = pool.shape[0]
+    tall = full // 5 if full % 80 == 0 else full // 2 // 16 * 16 if full % 32 == 0 else 16
     lanes = 4 * rows
     half, quart = predv.shape[0] // 2, predv.shape[0] // 4
     og = gp.shape[0]
@@ -57,8 +64,6 @@
         return (lax.rem(y_ + 2 * RING, RING) * 2 + xl_, ci)
 
     count = [0]
-    started = []
-
     def send(src, dst, dev):
         n = count[0]
         count[0] += 1
@@ -84,10 +89,20 @@
     for dev in greet:
         pl.semaphore_signal(barrier, inc=1, device_id=dev, device_id_type=MESH)
 
-    load_pool = pltpu.make_async_copy(cpool, pool, lsem.at[0])
+    load_pool = pltpu.make_async_copy(cpool.at[0:pm], pool.at[0:pm], lsem.at[0])
     load_pool.start()
     load_coef = pltpu.make_async_copy(coef, coefv, lsem.at[1])
     load_coef.start()
+
+    def over(n, body):
+        times = 3 if n % 3 == 0 else 1
+
+        def group(m, carry):
+            for k in range(times):
+                body((m * times + k) * 256)
+            return carry
+
+        lax.fori_loop(0, n // times, group, 0)
 
     def rows_at(k):
         return pl.ds(pl.multiple_of(k * rows, rows), rows)
@@ -109,6 +124,17 @@
     xall[0, rows_at(j), :] = dot(pick, bsel[...], TN).astype(BF16)
     tg[rows_at(j), :] = jnp.zeros((rows, tg.shape[1]), F32)
     tg[rows_at(j), 0:out] = tgt[...]
+
+    cbase = ci * n_pool
+    step_rows = 32
+
+    def build(m, carry):
+        r0 = pl.multiple_of(m * step_rows, step_rows)
+        at_row = lax.broadcasted_iota(jnp.int32, (step_rows, cen), 0) + (cbase + r0)
+        oht[pl.ds(r0, step_rows), :] = jnp.where(at_row == cidx[...], 1.0, 0.0).astype(BF16)
+        return carry
+
+    lax.fori_loop(0, pp // step_rows, build, 0)
 
     pl.semaphore_wait(barrier, len(greet))
 
@@ -160,16 +186,20 @@
                 mate[s, 0].wait_recv()
                 mate[s, 1].wait_recv()
 
-    cbase = ci * n_pool
-    step_rows = 32
-
-    def build(m, carry):
-        r0 = pl.multiple_of(m * step_rows, step_rows)
-        at_row = lax.broadcasted_iota(jnp.int32, (step_rows, cen), 0) + (cbase + r0)
-        oht[pl.ds(r0, step_rows), :] = jnp.where(at_row == cidx[...], 1.0, 0.0).astype(BF16)
-        return carry
-
-    lax.fori_loop(0, pp // step_rows, build, 0)
+    load_pool.wait()
+    last = ctail[...]
+    real = lax.broadcasted_iota(jnp.int32, last.shape, 0) < n_pool - pm
+    pool[pm:full, :] = jnp.where(real, last, jnp.zeros_like(last))
+
+    def squares(r0, n):
+        wide = pool[pl.ds(r0, n), :].astype(F32)
+        cs[pl.ds(r0, n), :] = jnp.broadcast_to(
+            jnp.sum(wide * wide, axis=1, keepdims=True), (n, 128)
+        )
+
+    over(pm // 256, lambda r0: squares(pl.multiple_of(r0, 256), 256))
+    squares(pm, full - pm)
+    kt[full:, :] = jnp.zeros_like(kt[full:, :])
     forward(0)
 
     load_coef.wait()
@@ -184,57 +214,28 @@
             coefb[...], oht[pl.ds(n, width), :], NT
         ).astype(BF16)
 
-    def permute_body(m, carry):
-        permute(m * 256, 256)
-        return carry
-
-    lax.fori_loop(0, pm // 256, permute_body, 0)
-    permute(pm, pp - pm)
-    forward(1)
-
-    load_pool.wait()
-    tailp[...] = jnp.zeros_like(tailp)
-    tailp[0 : n_pool - pm, :] = pool[pm:n_pool, :]
-
-    def squares(m, carry):
-        r0 = pl.multiple_of(m * 128, 128)
-        wide = pool[pl.ds(r0, 128), :].astype(F32)
-        cs[pl.ds(r0, 128), :] = jnp.broadcast_to(
-            jnp.sum(wide * wide, axis=1, keepdims=True), (128, 128)
-        )
-        return carry
-
-    lax.fori_loop(0, pm // 128, squares, 0)
-    wide_tail = tailp[...].astype(F32)
-    cs_tail = jnp.sum(wide_tail * wide_tail, axis=1, keepdims=True)
-    kt[pm:, :] = jnp.zeros_like(kt[pm:, :])
-
     def near(squared):
-        return jnp.exp(-jnp.sqrt(jnp.maximum(squared, 0.0))).astype(BF16)
+        floor = jnp.maximum(squared, 1e-30)
+        return jnp.exp2(floor * lax.rsqrt(floor) * -LOG2E).astype(BF16)
 
     def kernel_of(p0, n):
         width = n * lanes
         cols = slice(p0 * lanes, p0 * lanes + width)
         feats = xall[p0 : p0 + n].reshape(width, d)
         wide = feats.astype(F32)
-        square = wide * wide * 0.25
-        high = square.astype(BF16)
-        low = (square - high.astype(F32)).astype(BF16)
-        ones = jnp.ones((16, d), BF16)
-        row = (dot(ones, high, NT) + dot(ones, low, NT))[0:1, :]
+        size = jnp.sum(wide * wide, axis=1, keepdims=True) * 0.25
+        row = jnp.broadcast_to(size, (width, 128)).T[0:1, :]
 
         def body(m, carry):
-            r0 = pl.multiple_of(m * 256, 256)
-            both = dot(pool[pl.ds(r0, 256), :], xall[p0 : p0 + n].reshape(width, d), NT)
-            col = cs[pl.ds(r0, 256), :]
+            r0 = pl.multiple_of(m * tall, 16)
+            both = dot(pool[pl.ds(r0, tall), :], xall[p0 : p0 + n].reshape(width, d), NT)
+            col = cs[pl.ds(r0, tall), :]
             col = jnp.concatenate([col] * (width // 128), axis=1) if width > 128 else col[:, :width]
-            kt[pl.ds(r0, 256), cols] = near(row + col + both)
+            kt[pl.ds(r0, tall), cols] = near(row + col + both)
             return carry
 
-        lax.fori_loop(0, pm // 256, body, 0)
-        both = dot(tailp[...], feats, NT)
-        real = lax.broadcasted_iota(jnp.int32, both.shape, 0) < n_pool - pm
-        kt[pm : pm + 16, cols] = jnp.where(real, near(row + cs_tail + both), 0.0).astype(BF16)
+        for m in range(full // tall):
+            body(m, 0)
         predv[:, cols] = dot(coefp[...], kt[:, cols], NN)
 
     core_sent = {}
@@ -264,33 +265,34 @@
                     qsend.at[PLACE[s], k], qrecv.at[back, k], at(z + s, xd, c)
                 )
 
-    ready((0,))
-    kernel_of(0, 1)
-    share((0,))
+    cuts = (0, pm // 768 * 512, pm) if pm % 768 == 0 else (0, 0, pm)
+    over((cuts[1] - cuts[0]) // 256, lambda n0: permute(n0, 256))
+    forward(1)
+    over((cuts[2] - cuts[1]) // 256, lambda n0: permute(cuts[1] + n0, 256))
+    permute(pm, pp - pm)
+    ready((0, 1))
+    kernel_of(0, 2)
+    share((0, 1))
     forward(2)
-    ready((1, 7))
-    kernel_of(PLACE[1], 2)
-    share((1, 7))
-    spread((0,))
+    ready((7, 2))
+    kernel_of(2, 2)
+    share((7, 2))
+    spread((0, 1))
     forward(3)
-    ready((2, 6))
-    kernel_of(PLACE[2], 2)
-    share((2, 6))
-    spread((1, 7))
+    ready((6, 3))
+    kernel_of(4, 2)
+    share((6, 3))
+    spread((7, 2))
     forward(4)
-    ready((3, 5))
-    kernel_of(PLACE[3], 2)
-    share((3, 5))
-    spread((2, 6))
-    ready((4,))
-    kernel_of(1, 1)
-    share((4,))
-    spread((3, 5))
+    ready((5, 4))
+    kernel_of(6, 2)
+    share((5, 4))
+    spread((6, 3))
     if zs:
         for copy in tg_sent:
             copy.wait_recv()
     tt[...] = tg[...].T
-    spread((4,))
+    spread((5, 4))
 
     total = predv[quart_at(j), lane_of(0)]
     for s in (0, 1, 7, 2, 6, 3, 5, 4):
@@ -345,29 +347,26 @@
             else:
                 gpb[:, pl.ds(n0, width)] = (gp[:, pl.ds(n0, width)] + term).astype(BF16)
 
-        def body(m, carry):
-            part(m * 256, 256)
-            return carry
-
-        lax.fori_loop(0, pm // 256, body, 0)
+        over(pm // 256, lambda n0: part(n0, 256))
         part(pm, pp - pm)
 
-    res_ready((1, 7, 2, 6, 3, 5))
-    gradient(2, 6, True)
-    res_ready((4, 0))
-    gradient(0, 2, False)
-
-    def own_term(s, h):
-        col = lax.rem(y + s + RING, RING) * chunk + h * sub
-        return dot(gpb[...], oht[:, pl.ds(pl.multiple_of(col, 128), sub)], NN)
+    res_ready((0, 1, 7, 2, 6, 3))
+    gradient(0, 6, True)
+    res_ready((5, 4))
+    gradient(6, 2, False)
+
+    def own_term(s):
+        col = lax.rem(y + s + RING, RING) * chunk
+        return dot(gpb[...], oht[:, pl.ds(pl.multiple_of(col, 128), chunk)], NN)
 
     if ys:
         chain = {}
         for t in range(1, 5):
             s = 5 - t
+            own_terms = {1: own_term(s)}
+            own_terms[-1] = own_terms[1] if t == 1 else own_term(-s)
             for h in (0, 1):
-                terms = {1: own_term(s, h)}
-                terms[-1] = terms[1] if t == 1 else own_term(-s, h)
+                terms = {way: own_terms[way][:, h * sub : (h + 1) * sub] for way in (1, -1)}
                 for w, way in enumerate((1, -1)):
                     first = slice(0, cut) if way == 1 else slice(cut, og)
                     if t == 1:
@@ -390,8 +389,9 @@
                     chain[way, t, h] = send(
                         ysend.at[w, t - 1, h], yrecv.at[w, t - 1, h], at_y(y + way, xl)
                     )
+        own_here = own_term(0)
         for h in (0, 1):
-            fin[h] = own_term(0, h)
+            fin[h] = own_here[:, h * sub : (h + 1) * sub]
         for h in (0, 1):
             chain[1, 4, h].wait_recv()
             chain[-1, 4, h].wait_recv()
@@ -408,7 +408,7 @@
     else:
         for s in range(RING):
             for h in (0, 1):
-                grad[s, h] = own_term(s, h).astype(BF16)
+                grad[s, h] = own_term(s)[:, h * sub : (h + 1) * sub].astype(BF16)
 
     stores = []
 
@@ -476,19 +476,20 @@
     sub = chunk // 2
     vmem = pl.BlockSpec(memory_space=pltpu.VMEM)
     hbm = pl.BlockSpec(memory_space=pl.ANY)
+    tail = pl.BlockSpec((16, d), lambda i: (n_pool // 256 * 16, 0))
     grad, residual = pl.pallas_call(
         functools.partial(step_kernel, zs, ys),
         out_shape=(
             jax.ShapeDtypeStruct((og, cen), BF16),
             jax.ShapeDtypeStruct((rows, out), F32),
         ),
-        in_specs=[vmem, vmem, vmem, hbm, vmem, hbm],
+        grid=(1,),
+        in_specs=[vmem, vmem, vmem, hbm, tail, vmem, hbm],
         out_specs=(hbm, vmem),
         scratch_shapes=[
             pltpu.VMEM((up(bpool.shape[0], 16), d), BF16),
             pltpu.VMEM((RING, lanes, d), BF16),
-            pltpu.VMEM((n_pool, d), BF16),
-            pltpu.VMEM((16, d), BF16),
+            pltpu.VMEM((up(n_pool, 16), d), BF16),
             pltpu.VMEM((pp, 128), F32),
             pltpu.VMEM((pp, cen), BF16),
             pltpu.VMEM((out, cen), F32),
@@ -523,7 +524,7 @@
         ),
         name="regression_step",
     )(
-        bidx.reshape(1, rows), bpool, cidx.reshape(1, cen), cpool, tgt, coef.T,
+        bidx.reshape(1, rows), bpool, cidx.reshape(1, cen), cpool, cpool, tgt, coef.T,
     )
     batch_total = rows * lax.axis_size("batch") * lax.axis_size("centre")
     step_size = 8.0 / math.sqrt(batch_total)

time: 129 us -> 115 us (0.89)
  Pallas kernels: 124 us -> 109 us
    pallas_call x1, Pallas kernels: 124 us -> 109 us  [on_device(): pl.pallas_call(functools.partial(step_kernel, zs, ys), out_shape=(jax.Sha...]
where the time goes in v2:
time: 115 us
  Pallas kernels  109 us (95%)
  other arithmetic  3.97 us (3%)
    pallas_call x1, Pallas kernels, on_device(): pl.pallas_call(functools.partial(step_kernel, zs, ys), out_shape=(jax.Sha...  109 us
    sub x1, other arithmetic, on_device(): updated = coef - step_size * grad[:out].astype(F32).T  3.97 us

profile of v2, /device:TPU:8, one launch (start us, length us, event | category | flops | bytes accessed | tf_op | source)
XLA Modules:
  0.0 114.6 jit_solution(14959653767653615526)
XLA Ops:
  0.6 109.3 %regression_step.1 = (bf16[304,2048]{1,0:T(8,128)(2,1)}, f32[32,301]{1,0:T(8,128)}) custom-call(s32[1,32]{1,0:T(1,128)} %bitcast.7, bf16[41,1024]{1,0:T(8,128)(2,1)} %refs_1_.1, s32[1,2048]{1,0:T(1,128)} %bitcast.6, bf16[2305,1024]{1,0:T(8,128)(2,1)} %refs_4_.1, bf16[2305,1024]{1,0:T(8,128)(2,1)} %refs_4_.1, f32[32,301]{1,0:T(8,128)} %refs_5_.1, ...), custom_call_target="tpu_custom_call" | custom-call | tf_op jit(solution)/shard_map/regression_step/pallas_call | solution.py:480
  110.0 0.0 copy-start
  110.0 4.0 %bitcast_subtract_fusion = f32[2048,301]{0,1:T(8,128)} fusion(f32[2048,301]{0,1:T(8,128)} %param.11, bf16[304,2048]{1,0:T(8,128)(2,1)} %get-tuple-element.4), kind=kLoop, calls=%fused_computation | loop fusion | flops 1849344 | bytes 6164480 | tf_op jit(solution)/shard_map/sub | solution.py:531
  114.0 0.0 copy-done
  114.0 0.6 copy.9
Async XLA Ops:
  110.0 4.0 %copy-start = (f32[32,301]{1,0:T(8,128)S(1)}, f32[32,301]{1,0:T(8,128)}, u32[]{:S(2)}) copy-start(f32[32,301]{1,0:T(8,128)} %get-tuple-element.9) | copy-start | bytes 115588

commit v3 on v2

--- a/solution.py
+++ b/solution.py
@@ -16,7 +16,7 @@
 NN = (((1,), (0,)), ((), ()))
 TN = (((0,), (0,)), ((), ()))
 PLACE = (0, 1, 3, 5, 7, 6, 4, 2)
-COPIES = 128
+COPIES = 176
 LOG2E = 1.4426950408889634
 
 
@@ -35,7 +35,7 @@
 def inner_kernel(
     started, zs, ys, bidx, bpool, cidx, cpool, ctail, tgt, coef, grad_out, res_out,
     bsel, xall, pool, cs, oht, coefv, coefb, coefp, kt, predv, psend, precv,
-    qsend, qrecv, tg, tt, res, rq, rt, gp, gpb, ysend, yrecv, fin, xsend, xrecv, grad,
+    qsend, qrecv, tg, tt, res, rq, rt, gp, gpb, terms, xps, xpr, yps, ypr, yqs, yqr, xsend, xrecv, grad,
     ssem, rsem, lsem, osem,
 ):
     bi = lax.axis_index("batch")
@@ -53,7 +53,10 @@
     lanes = 4 * rows
     half, quart = predv.shape[0] // 2, predv.shape[0] // 4
     og = gp.shape[0]
-    cut = up(og // 2, 16)
+    top = xps.shape[1]
+    mid_p = up(top // 2, 16)
+    mid_q = top + up((og - top) // 2, 16)
+    split = up((og + og - top) // 2, 16)
     chunk = cen // RING
     sub = chunk // 2
 
@@ -146,8 +149,6 @@
         for way, slot in ((1, RING - 1), (-1, 1)):
             ring[way, 1, 0] = send(own, xall.at[PLACE[slot], rows_at(j)], at(z + way, x, c))
         mate[0, 0] = send(own, own, partner)
-        mine = tg.at[rows_at(j)]
-        tg_sent = [send(mine, mine, dev) for dev in (partner, facing, across)]
 
     def slot_of(way, level):
         return RING - level if way == 1 else level
@@ -270,6 +271,9 @@
     forward(1)
     over((cuts[2] - cuts[1]) // 256, lambda n0: permute(cuts[1] + n0, 256))
     permute(pm, pp - pm)
+    if zs:
+        mine = tg.at[rows_at(j)]
+        tg_sent = [send(mine, mine, dev) for dev in (partner, facing, across)]
     ready((0, 1))
     kernel_of(0, 2)
     share((0, 1))
@@ -306,29 +310,47 @@
     if zs:
         quarter = res.at[0, quart_at(j)]
         res_x = send(quarter, quarter, facing)
-        far = (4, 3, 5, 2, 6, 1, 7)
         res_z = {}
-        for s in far:
-            res_z[s, 0] = send(
-                quarter, res.at[PLACE[(RING - s) % RING], quart_at(j)], at(z + s, x, c)
+
+        def res_send(way, dist, stream, hops):
+            rows_of = quart_at((j, jx)[stream])
+            here = PLACE[(-way * (dist - hops)) % RING]
+            there = PLACE[(-way * dist) % RING]
+            res_z[way, dist, stream] = send(
+                res.at[here, rows_of], res.at[there, rows_of], at(z + way * hops, x, c)
             )
+
+        for dist in (2, 1):
+            for way in (1, -1):
+                res_send(way, dist, 0, dist)
         res_x.wait_recv()
-        other = res.at[0, quart_at(jx)]
-        for s in far:
-            res_z[s, 1] = send(
-                other, res.at[PLACE[(RING - s) % RING], quart_at(jx)], at(z + s, x, c)
-            )
+        for dist in (2, 1):
+            for way in (1, -1):
+                res_send(way, dist, 1, dist)
         res_mate = {}
-        block = res.at[0, half_at(c)]
-        res_mate[0] = send(block, block, partner)
+
+        def res_pass(slot):
+            block = res.at[PLACE[slot], half_at(c)]
+            res_mate[slot] = send(block, block, partner)
+
+        res_pass(0)
         wide_q = rq.at[quart_at(j)]
         rq_sent = [send(wide_q, wide_q, dev) for dev in (partner, facing, across)]
-        for s in (1, 7, 2, 6, 3, 5, 4):
-            back = (RING - s) % RING
-            res_z[back, 0].wait_recv()
-            res_z[back, 1].wait_recv()
-            block = res.at[PLACE[s], half_at(c)]
-            res_mate[s] = send(block, block, partner)
+        for stream in (0, 1):
+            for way in (1, -1):
+                res_z[way, 2, stream].wait_recv()
+                if (way == 1) == (stream == 0):
+                    res_send(way, 4, stream, 2)
+                res_send(way, 3, stream, 1)
+        for dist in (1, 2, 3):
+            for way in (1, -1):
+                if dist != 2:
+                    res_z[way, dist, 0].wait_recv()
+                    res_z[way, dist, 1].wait_recv()
+                res_pass((-way * dist) % RING)
+        res_z[1, 4, 0].wait_recv()
+        res_z[-1, 4, 1].wait_recv()
+        res_pass(4)
 
     def res_ready(slots):
         if zs:
@@ -359,52 +381,95 @@
         col = lax.rem(y + s + RING, RING) * chunk
         return dot(gpb[...], oht[:, pl.ds(pl.multiple_of(col, 128), chunk)], NN)
 
+    rows_p, rows_q = slice(0, top), slice(top, og)
+    first_p = {1: slice(0, mid_p), -1: slice(mid_p, top)}
+    first_q = {1: slice(top, mid_q), -1: slice(mid_q, og)}
     if ys:
+        beside = at_y(y, 1 - xl)
         chain = {}
-        for t in range(1, 5):
-            s = 5 - t
-            own_terms = {1: own_term(s)}
-            own_terms[-1] = own_terms[1] if t == 1 else own_term(-s)
+        swap = {}
+
+        def term(s):
+            whole = own_term(s)
             for h in (0, 1):
-                terms = {way: own_terms[way][:, h * sub : (h + 1) * sub] for way in (1, -1)}
-                for w, way in enumerate((1, -1)):
-                    first = slice(0, cut) if way == 1 else slice(cut, og)
-                    if t == 1:
-                        ysend[w, 0, h, first, :] = terms[way][first].astype(BF16)
-                        chain[way, t, h] = send(
-                            ysend.at[w, 0, h, first], yrecv.at[w, 0, h, first], at_y(y + way, xl)
-                        )
-                        continue
-                    chain[way, t - 1, h].wait_recv()
+                terms[s % RING, h] = whole[:, h * sub : (h + 1) * sub]
+            xps[s % RING] = terms[s % RING, 1 - xl, rows_p, :].astype(BF16)
+            swap[s % RING] = send(xps.at[s % RING], xpr.at[s % RING], beside)
+
+        def pass_on(kind, t, own, part, first, buffer, landed, h):
+            for w, way in enumerate((1, -1)):
+                s = (way * (5 - t)) % RING
+                mine = own(s)
+                base = part.start
+                near_rows = slice(first[way].start - base, first[way].stop - base)
+                out_at, in_at = buffer.at[w, t - 1, h], landed.at[w, t - 1, h]
+                if t == 1:
+                    out_at, in_at = out_at.at[near_rows], in_at.at[near_rows]
+                    buffer[w, 0, h, near_rows, :] = mine[near_rows].astype(BF16)
+                else:
+                    chain[kind, way, t - 1, h].wait_recv()
                     if t == 2:
-                        rest = slice(cut, og) if way == 1 else slice(0, cut)
-                        ysend[w, 1, h, first, :] = (
-                            terms[way][first] + yrecv[w, 0, h, first, :].astype(F32)
+                        other = first[-way]
+                        far_rows = slice(other.start - base, other.stop - base)
+                        buffer[w, 1, h, near_rows, :] = (
+                            mine[near_rows] + landed[w, 0, h, near_rows, :].astype(F32)
                         ).astype(BF16)
-                        ysend[w, 1, h, rest, :] = terms[way][rest].astype(BF16)
+                        buffer[w, 1, h, far_rows, :] = mine[far_rows].astype(BF16)
                     else:
-                        ysend[w, t - 1, h] = (
-                            terms[way] + yrecv[w, t - 2, h].astype(F32)
+                        buffer[w, t - 1, h] = (
+                            mine + landed[w, t - 2, h].astype(F32)
                         ).astype(BF16)
-                    chain[way, t, h] = send(
-                        ysend.at[w, t - 1, h], yrecv.at[w, t - 1, h], at_y(y + way, xl)
-                    )
-        own_here = own_term(0)
+                chain[kind, way, t, h] = send(out_at, in_at, at_y(y + way, xl))
+
+        def pass_q(t):
+            for h in (0, 1):
+                pass_on(
+                    "q", t, lambda s, h=h: terms[s, h, rows_q, :], rows_q, first_q, yqs, yqr, h
+                )
+
+        def both_x(s):
+            if s in swap:
+                swap.pop(s).wait_recv()
+                terms[s, xl, rows_p, :] += xpr[s].astype(F32)
+            return terms[s, xl, rows_p, :]
+
+        def pass_p(t):
+            pass_on("p", t, both_x, rows_p, first_p, yps, ypr, 0)
+
+        term(4)
+        pass_q(1)
+        term(3)
+        term(5)
+        pass_q(2)
+        pass_p(1)
+        term(2)
+        term(6)
+        pass_q(3)
+        pass_p(2)
+        term(1)
+        term(7)
+        pass_q(4)
+        term(0)
+        pass_p(3)
         for h in (0, 1):
-            fin[h] = own_here[:, h * sub : (h + 1) * sub]
-        for h in (0, 1):
-            chain[1, 4, h].wait_recv()
-            chain[-1, 4, h].wait_recv()
-            fin[h] = fin[h] + yrecv[0, 3, h].astype(F32) + yrecv[1, 3, h].astype(F32)
-        xsend[...] = fin[1 - xl].astype(BF16)
-        swap = send(xsend, xrecv, at_y(y, 1 - xl))
-        swap.wait_recv()
-        grad[0, xl] = (fin[xl] + xrecv[...].astype(F32)).astype(BF16)
+            chain["q", 1, 4, h].wait_recv()
+            chain["q", -1, 4, h].wait_recv()
+            terms[0, h, rows_q, :] += yqr[0, 3, h].astype(F32) + yqr[1, 3, h].astype(F32)
+        xsend[...] = terms[0, 1 - xl, rows_q, :].astype(BF16)
+        swap_q = send(xsend, xrecv, beside)
+        pass_p(4)
+        sum_p = both_x(0)
+        chain["p", 1, 4, 0].wait_recv()
+        chain["p", -1, 4, 0].wait_recv()
+        sum_p = sum_p + ypr[0, 3, 0].astype(F32) + ypr[1, 3, 0].astype(F32)
+        grad[0, xl, rows_p, :] = sum_p.astype(BF16)
+        swap_q.wait_recv()
+        grad[0, xl, rows_q, :] = (terms[0, xl, rows_q, :] + xrecv[...].astype(F32)).astype(BF16)
         own = grad.at[0, xl]
         back = {}
         for way, slot in ((1, RING - 1), (-1, 1)):
             back[way, 1, 0] = send(own, grad.at[slot, xl], at_y(y + way, xl))
-        cross_l = send(own, own, at_y(y, 1 - xl))
+        cross_l = send(own, own, beside)
     else:
         for s in range(RING):
             for h in (0, 1):
@@ -425,29 +490,55 @@
     if ys:
         store(0, xl)
         cross_l.wait_recv()
-        other = grad.at[0, 1 - xl]
         for way, slot in ((1, RING - 1), (-1, 1)):
-            back[way, 1, 1] = send(other, grad.at[slot, 1 - xl], at_y(y + way, xl))
+            back[way, 1, 1] = send(
+                grad.at[0, 1 - xl, rows_q], grad.at[slot, 1 - xl, rows_q], at_y(y + way, xl)
+            )
         store(0, 1 - xl)
-        for level in range(1, 5):
-            for stream, h in ((0, xl), (1, 1 - xl)):
+        beside_sent = {}
+        last_way = {1: slice(0, split), -1: slice(split, og)}
+
+        def give(slot):
+            block = grad.at[slot, xl, rows_p]
+            beside_sent[slot] = send(block, block, beside)
+            store(slot, xl)
+
+        for level in range(1, 4):
+            for way in (1, -1):
+                slot = slot_of(way, level)
+                nxt = slot_of(way, level + 1)
+                back[way, level, 0].wait_recv()
+                part = last_way[way] if level == 3 else slice(0, og)
+                back[way, level + 1, 0] = send(
+                    grad.at[slot, xl, part], grad.at[nxt, xl, part], at_y(y + way, xl)
+                )
+                give(slot)
+            for way in (1, -1):
+                slot = slot_of(way, level)
+                nxt = slot_of(way, level + 1)
+                back[way, level, 1].wait_recv()
+                if level < 3 or way == -1:
+                    back[way, level + 1, 1] = send(
+                        grad.at[slot, 1 - xl, rows_q], grad.at[nxt, 1 - xl, rows_q],
+                        at_y(y + way, xl),
+                    )
+            if level == 1 and zs:
+                for copy in rq_sent:
+                    copy.wait_recv()
+                rt[...] = rq[...].T
+                res_out[...] = rt[rows_at(j), 0:out]
+            if level > 1:
                 for way in (1, -1):
-                    straight = (way == 1) == (stream == 0)
-                    if level == 4 and not straight:
-                        continue
-                    back[way, level, stream].wait_recv()
-                    slot = slot_of(way, level)
-                    if level < 3 or (level == 3 and straight):
-                        back[way, level + 1, stream] = send(
-                            grad.at[slot, h], grad.at[slot_of(way, level + 1), h],
-                            at_y(y + way, xl),
-                        )
-                    store(slot, h)
-                    if level == 1 and stream == 0 and way == 1 and zs:
-                        for copy in rq_sent:
-                            copy.wait_recv()
-                        rt[...] = rq[...].T
-                        res_out[...] = rt[rows_at(j), 0:out]
+                    slot = slot_of(way, level - 1)
+                    beside_sent[slot].wait_recv()
+                    store(slot, 1 - xl)
+        back[1, 4, 0].wait_recv()
+        back[-1, 4, 0].wait_recv()
+        give(4)
+        back[-1, 4, 1].wait_recv()
+        for slot in (5, 3, 4):
+            beside_sent[slot].wait_recv()
+            store(slot, 1 - xl)
     else:
         for s in range(RING):
             for h in (0, 1):
@@ -474,6 +565,7 @@
     wide = up(outp, 128)
     chunk = cen // RING
     sub = chunk // 2
+    top = up(og * 9 // 16, 16)
     vmem = pl.BlockSpec(memory_space=pltpu.VMEM)
     hbm = pl.BlockSpec(memory_space=pl.ANY)
     tail = pl.BlockSpec((16, d), lambda i: (n_pool // 256 * 16, 0))
@@ -508,11 +600,15 @@
             pltpu.VMEM((lanes, outp), F32),
             pltpu.VMEM((og, pp), F32),
             pltpu.VMEM((og, pp), BF16),
-            pltpu.VMEM((2, 4, 2, og, sub), BF16),
-            pltpu.VMEM((2, 4, 2, og, sub), BF16),
-            pltpu.VMEM((2, og, sub), F32),
-            pltpu.VMEM((og, sub), BF16),
-            pltpu.VMEM((og, sub), BF16),
+            pltpu.VMEM((RING, 2, og, sub), F32),
+            pltpu.VMEM((RING, top, sub), BF16),
+            pltpu.VMEM((RING, top, sub), BF16),
+            pltpu.VMEM((2, 4, 1, top, sub), BF16),
+            pltpu.VMEM((2, 4, 1, top, sub), BF16),
+            pltpu.VMEM((2, 4, 2, og - top, sub), BF16),
+            pltpu.VMEM((2, 4, 2, og - top, sub), BF16),
+            pltpu.VMEM((og - top, sub), BF16),
+            pltpu.VMEM((og - top, sub), BF16),
             pltpu.VMEM((RING, 2, og, sub), BF16),
             pltpu.SemaphoreType.DMA((COPIES,)),
             pltpu.SemaphoreType.DMA((COPIES,)),
@@ -520,7 +616,7 @@
             pltpu.SemaphoreType.DMA((2 * RING,)),
         ],
         compiler_params=pltpu.CompilerParams(
-            collective_id=0, has_side_effects=True, vmem_limit_bytes=62 * 1024 * 1024
+            collective_id=0, has_side_effects=True, vmem_limit_bytes=48 * 1024 * 1024
         ),
         name="regression_step",
     )(

time: 115 us -> 114 us (level)
  local copies, waits for them, and re-layouts: 0.62 us -> 5.36 us
  Pallas kernels: 109 us -> 106 us
  other arithmetic: 3.97 us -> 1.85 us
    unnamed x3 -> x11, local copies, waits for them, and re-layouts: 0.62 us -> 5.36 us
    pallas_call x1, Pallas kernels: 109 us -> 106 us  [on_device(): pl.pallas_call(functools.partial(step_kernel, zs, ys), out_shape=(jax.Sha...]
    sub x1, other arithmetic: 3.97 us -> 1.85 us  [on_device(): updated = coef - step_size * grad[:out].astype(F32).T]
where the time goes in v3:
time: 114 us
  Pallas kernels  106 us (93%)
  local copies, waits for them, and re-layouts  5.36 us (5%)
  other arithmetic  1.85 us (2%)
    pallas_call x1, Pallas kernels, on_device(): pl.pallas_call(functools.partial(step_kernel, zs, ys), out_shape=(jax.Sha...  106 us
    unnamed x11, local copies, waits for them, and re-layouts  5.36 us

profile of v3, /device:TPU:8, one launch (start us, length us, event | category | flops | bytes accessed | tf_op | source)
XLA Modules:
  0.0 114.0 jit_solution(4135407595848204273)
XLA Ops:
  0.6 0.0 copy-start
  0.6 1.7 %copy-done = f32[2048,301]{0,1:T(8,128)S(1)} copy-done((f32[2048,301]{0,1:T(8,128)S(1)}, f32[2048,301]{0,1:T(8,128)}, u32[]{:S(2)}) %copy-start) | copy-done | bytes 2465816
  2.3 0.0 copy-start.1
  2.3 0.9 copy-done.1
  3.2 0.0 copy-start.2
  3.2 0.8 copy-done.2
  4.0 0.0 copy-start.3
  4.0 0.7 copy-done.3
  4.7 0.0 copy-start.4
  4.7 0.7 copy-done.4
  5.4 106.2 %regression_step.1 = (bf16[304,2048]{1,0:T(8,128)(2,1)S(1)}, f32[32,301]{1,0:T(8,128)S(1)}) custom-call(s32[1,32]{1,0:T(1,128)S(1)} %bitcast.7, bf16[41,1024]{1,0:T(8,128)(2,1)S(1)} %copy-done.1, s32[1,2048]{1,0:T(1,128)S(1)} %bitcast.6, bf16[2305,1024]{1,0:T(8,128)(2,1)} %refs_4_.1, bf16[2305,1024]{1,0:T(8,128)(2,1)} %refs_4_.1, f32[32,301]{1,0:T(8,128)S(1)} %copy-done.2, ...), custom_call_target="tpu_custom_call" | custom-call | tf_op jit(solution)/shard_map/regression_step/pallas_call | solution.py:572
  111.6 1.8 %bitcast_subtract_fusion = f32[2048,301]{0,1:T(8,128)} fusion(f32[2048,301]{0,1:T(8,128)S(1)} %copy-done, bf16[304,2048]{1,0:T(8,128)(2,1)S(1)} %get-tuple-element.4), kind=kLoop, calls=%fused_computation | loop fusion | flops 1849344 | bytes 6164480 | tf_op jit(solution)/shard_map/sub | solution.py:627
  113.4 0.6 copy.9
Async XLA Ops:
  0.6 1.7 %copy-start = (f32[2048,301]{0,1:T(8,128)S(1)}, f32[2048,301]{0,1:T(8,128)}, u32[]{:S(2)}) copy-start(f32[2048,301]{0,1:T(8,128)} %param.11) | copy-start | bytes 7397380
  2.3 0.9 copy-start.1
  3.2 0.8 copy-start.2
  4.0 0.7 copy-start.3
  4.7 0.7 copy-start.4

commit v4 on v3

--- a/solution.py
+++ b/solution.py
@@ -49,14 +49,13 @@
     pp = kt.shape[0]
     pm = n_pool // 256 * 256
     full = pool.shape[0]
-    tall = full // 5 if full % 80 == 0 else full // 2 // 16 * 16 if full % 32 == 0 else 16
+    tall = full // 5 if full % 80 == 0 else 16
     lanes = 4 * rows
     half, quart = predv.shape[0] // 2, predv.shape[0] // 4
     og = gp.shape[0]
     top = xps.shape[1]
     mid_p = up(top // 2, 16)
     mid_q = top + up((og - top) // 2, 16)
-    split = up((og + og - top) // 2, 16)
     chunk = cen // RING
     sub = chunk // 2
 
@@ -219,7 +218,7 @@
         floor = jnp.maximum(squared, 1e-30)
         return jnp.exp2(floor * lax.rsqrt(floor) * -LOG2E).astype(BF16)
 
-    def kernel_of(p0, n):
+    def kernel_of(p0, n, level=None):
         width = n * lanes
         cols = slice(p0 * lanes, p0 * lanes + width)
         feats = xall[p0 : p0 + n].reshape(width, d)
@@ -227,16 +226,14 @@
         size = jnp.sum(wide * wide, axis=1, keepdims=True) * 0.25
         row = jnp.broadcast_to(size, (width, 128)).T[0:1, :]
 
-        def body(m, carry):
-            r0 = pl.multiple_of(m * tall, 16)
-            both = dot(pool[pl.ds(r0, tall), :], xall[p0 : p0 + n].reshape(width, d), NT)
-            col = cs[pl.ds(r0, tall), :]
+        for r0 in range(0, full, tall):
+            r1 = r0 + tall
+            both = dot(pool[r0:r1, :], xall[p0 : p0 + n].reshape(width, d), NT)
+            col = cs[r0:r1, :]
             col = jnp.concatenate([col] * (width // 128), axis=1) if width > 128 else col[:, :width]
-            kt[pl.ds(r0, tall), cols] = near(row + col + both)
-            return carry
-
-        for m in range(full // tall):
-            body(m, 0)
+            kt[r0:r1, cols] = near(row + col + both)
+            if r0 == tall and level is not None:
+                forward(level)
         predv[:, cols] = dot(coefp[...], kt[:, cols], NN)
 
     core_sent = {}
@@ -275,14 +272,12 @@
         mine = tg.at[rows_at(j)]
         tg_sent = [send(mine, mine, dev) for dev in (partner, facing, across)]
     ready((0, 1))
-    kernel_of(0, 2)
+    kernel_of(0, 2, 2)
     share((0, 1))
-    forward(2)
     ready((7, 2))
-    kernel_of(2, 2)
+    kernel_of(2, 2, 3)
     share((7, 2))
     spread((0, 1))
-    forward(3)
     ready((6, 3))
     kernel_of(4, 2)
     share((6, 3))
@@ -463,13 +458,29 @@
         chain["p", -1, 4, 0].wait_recv()
         sum_p = sum_p + ypr[0, 3, 0].astype(F32) + ypr[1, 3, 0].astype(F32)
         grad[0, xl, rows_p, :] = sum_p.astype(BF16)
+        back = {}
+
+        def copy_back(part, way, level):
+            h = 1 - xl if part == "b" else xl
+            rows_of = rows_p if part == "p" else rows_q
+            here = slot_of(way, level - 1) % RING
+            back[part, way, level] = send(
+                grad.at[here, h, rows_of], grad.at[slot_of(way, level), h, rows_of],
+                at_y(y + way, xl),
+            )
+
+        def give(slot, rows_of=rows_p):
+            block = grad.at[slot, xl, rows_of]
+            return send(block, block, beside)
+
+        copy_back("p", 1, 1)
+        copy_back("p", -1, 1)
+        beside_sent = {0: give(0)}
         swap_q.wait_recv()
         grad[0, xl, rows_q, :] = (terms[0, xl, rows_q, :] + xrecv[...].astype(F32)).astype(BF16)
-        own = grad.at[0, xl]
-        back = {}
-        for way, slot in ((1, RING - 1), (-1, 1)):
-            back[way, 1, 0] = send(own, grad.at[slot, xl], at_y(y + way, xl))
-        cross_l = send(own, own, beside)
+        beside_q = give(0, rows_q)
+        copy_back("q", 1, 1)
+        copy_back("q", -1, 1)
     else:
         for s in range(RING):
             for h in (0, 1):
@@ -489,54 +500,29 @@
 
     if ys:
         store(0, xl)
-        cross_l.wait_recv()
-        for way, slot in ((1, RING - 1), (-1, 1)):
-            back[way, 1, 1] = send(
-                grad.at[0, 1 - xl, rows_q], grad.at[slot, 1 - xl, rows_q], at_y(y + way, xl)
-            )
+        beside_q.wait_recv()
+        copy_back("b", 1, 1)
+        copy_back("b", -1, 1)
+        beside_sent[0].wait_recv()
         store(0, 1 - xl)
-        beside_sent = {}
-        last_way = {1: slice(0, split), -1: slice(split, og)}
-
-        def give(slot):
-            block = grad.at[slot, xl, rows_p]
-            beside_sent[slot] = send(block, block, beside)
-            store(slot, xl)
-
-        for level in range(1, 4):
-            for way in (1, -1):
-                slot = slot_of(way, level)
-                nxt = slot_of(way, level + 1)
-                back[way, level, 0].wait_recv()
-                part = last_way[way] if level == 3 else slice(0, og)
-                back[way, level + 1, 0] = send(
-                    grad.at[slot, xl, part], grad.at[nxt, xl, part], at_y(y + way, xl)
-                )
-                give(slot)
-            for way in (1, -1):
-                slot = slot_of(way, level)
-                nxt = slot_of(way, level + 1)
-                back[way, level, 1].wait_recv()
-                if level < 3 or way == -1:
-                    back[way, level + 1, 1] = send(
-                        grad.at[slot, 1 - xl, rows_q], grad.at[nxt, 1 - xl, rows_q],
-                        at_y(y + way, xl),
-                    )
+        for level in range(1, 5):
+            for part in ("p", "q", "b"):
+                only = 1 if part == "p" else -1
+                for way in (1, -1) if level < 4 else (only,):
+                    slot = slot_of(way, level)
+                    back[part, way, level].wait_recv()
+                    if level < 3 or (level == 3 and way == only):
+                        copy_back(part, way, level + 1)
+                    if part == "p":
+                        beside_sent[slot] = give(slot)
+                    elif part == "q":
+                        store(slot, xl)
             if level == 1 and zs:
                 for copy in rq_sent:
                     copy.wait_recv()
                 rt[...] = rq[...].T
                 res_out[...] = rt[rows_at(j), 0:out]
-            if level > 1:
-                for way in (1, -1):
-                    slot = slot_of(way, level - 1)
-                    beside_sent[slot].wait_recv()
-                    store(slot, 1 - xl)
-        back[1, 4, 0].wait_recv()
-        back[-1, 4, 0].wait_recv()
-        give(4)
-        back[-1, 4, 1].wait_recv()
-        for slot in (5, 3, 4):
+        for slot in (7, 1, 6, 2, 5, 3, 4):
             beside_sent[slot].wait_recv()
             store(slot, 1 - xl)
     else:

time: 114 us -> 113 us (level)
  the two profiles are of different devices: /device:TPU:8 before, /device:TPU:4 now
where the time goes in v4:
time: 113 us; the launch traced here: 112 us
  Pallas kernels  104 us (92%)
  local copies, waits for them, and re-layouts  5.36 us (5%)
  other arithmetic  1.85 us (2%)
    pallas_call x1, Pallas kernels, on_device(): pl.pallas_call(functools.partial(step_kernel, zs, ys), out_shape=(jax.Sha...  104 us
    unnamed x11, local copies, waits for them, and re-layouts  5.36 us

profile of v4, /device:TPU:4, one launch (start us, length us, event | category | flops | bytes accessed | tf_op | source)
XLA Modules:
  0.0 112.3 jit_solution(1795850501575801634)
XLA Ops:
  0.6 0.0 copy-start
  0.6 1.7 %copy-done = f32[2048,301]{0,1:T(8,128)S(1)} copy-done((f32[2048,301]{0,1:T(8,128)S(1)}, f32[2048,301]{0,1:T(8,128)}, u32[]{:S(2)}) %copy-start) | copy-done | bytes 2465816
  2.3 0.0 copy-start.1
  2.3 0.9 copy-done.1
  3.2 0.0 copy-start.2
  3.2 0.8 copy-done.2
  4.0 0.0 copy-start.3
  4.0 0.7 copy-done.3
  4.7 0.0 copy-start.4
  4.7 0.7 copy-done.4
  5.4 104.4 %regression_step.1 = (bf16[304,2048]{1,0:T(8,128)(2,1)S(1)}, f32[32,301]{1,0:T(8,128)S(1)}) custom-call(s32[1,32]{1,0:T(1,128)S(1)} %bitcast.7, bf16[41,1024]{1,0:T(8,128)(2,1)S(1)} %copy-done.1, s32[1,2048]{1,0:T(1,128)S(1)} %bitcast.6, bf16[2305,1024]{1,0:T(8,128)(2,1)} %refs_4_.1, bf16[2305,1024]{1,0:T(8,128)(2,1)} %refs_4_.1, f32[32,301]{1,0:T(8,128)S(1)} %copy-done.2, ...), custom_call_target="tpu_custom_call" | custom-call | tf_op jit(solution)/shard_map/regression_step/pallas_call | solution.py:558
  109.8 1.8 %bitcast_subtract_fusion = f32[2048,301]{0,1:T(8,128)} fusion(f32[2048,301]{0,1:T(8,128)S(1)} %copy-done, bf16[304,2048]{1,0:T(8,128)(2,1)S(1)} %get-tuple-element.4), kind=kLoop, calls=%fused_computation | loop fusion | flops 1849344 | bytes 6164480 | tf_op jit(solution)/shard_map/sub | solution.py:613
  111.6 0.6 copy.9
Async XLA Ops:
  0.6 1.7 %copy-start = (f32[2048,301]{0,1:T(8,128)S(1)}, f32[2048,301]{0,1:T(8,128)}, u32[]{:S(2)}) copy-start(f32[2048,301]{0,1:T(8,128)} %param.11) | copy-start | bytes 7397380
  2.3 0.9 copy-start.1
  3.2 0.8 copy-start.2
  4.0 0.7 copy-start.3
  4.7 0.7 copy-start.4

commit v5 on v4

--- a/solution.py
+++ b/solution.py
@@ -602,7 +602,7 @@
             pltpu.SemaphoreType.DMA((2 * RING,)),
         ],
         compiler_params=pltpu.CompilerParams(
-            collective_id=0, has_side_effects=True, vmem_limit_bytes=48 * 1024 * 1024
+            collective_id=0, has_side_effects=True, vmem_limit_bytes=62 * 1024 * 1024
         ),
         name="regression_step",
     )(

time: 113 us -> 111 us (0.982)
  local copies, waits for them, and re-layouts: 5.36 us -> 0.62 us
  other arithmetic: 1.85 us -> 3.97 us
  Pallas kernels: 104 us -> 106 us
    unnamed x11 -> x3, local copies, waits for them, and re-layouts: 5.36 us -> 0.62 us
    sub x1, other arithmetic: 1.85 us -> 3.97 us  [on_device(): updated = coef - step_size * grad[:out].astype(F32).T]
    pallas_call x1, Pallas kernels: 104 us -> 106 us  [on_device(): pl.pallas_call(functools.partial(step_kernel, zs, ys), out_shape=(jax.Sha...]
where the time goes in v5:
time: 111 us
  Pallas kernels  106 us (95%)
  other arithmetic  3.97 us (4%)
    pallas_call x1, Pallas kernels, on_device(): pl.pallas_call(functools.partial(step_kernel, zs, ys), out_shape=(jax.Sha...  106 us
    sub x1, other arithmetic, on_device(): updated = coef - step_size * grad[:out].astype(F32).T  3.97 us

profile of v5, /device:TPU:4, one launch (start us, length us, event | category | flops | bytes accessed | tf_op | source)
XLA Modules:
  0.0 111.1 jit_solution(2192812353503653617)
XLA Ops:
  0.6 105.9 %regression_step.1 = (bf16[304,2048]{1,0:T(8,128)(2,1)}, f32[32,301]{1,0:T(8,128)}) custom-call(s32[1,32]{1,0:T(1,128)} %bitcast.7, bf16[41,1024]{1,0:T(8,128)(2,1)} %refs_1_.1, s32[1,2048]{1,0:T(1,128)} %bitcast.6, bf16[2305,1024]{1,0:T(8,128)(2,1)} %refs_4_.1, bf16[2305,1024]{1,0:T(8,128)(2,1)} %refs_4_.1, f32[32,301]{1,0:T(8,128)} %refs_5_.1, ...), custom_call_target="tpu_custom_call" | custom-call | tf_op jit(solution)/shard_map/regression_step/pallas_call | solution.py:558
  106.5 0.0 copy-start
  106.5 4.0 %bitcast_subtract_fusion = f32[2048,301]{0,1:T(8,128)} fusion(f32[2048,301]{0,1:T(8,128)} %param.11, bf16[304,2048]{1,0:T(8,128)(2,1)} %get-tuple-element.4), kind=kLoop, calls=%fused_computation | loop fusion | flops 1849344 | bytes 6164480 | tf_op jit(solution)/shard_map/sub | solution.py:613
  110.5 0.0 copy-done
  110.5 0.6 copy.9
Async XLA Ops:
  106.5 4.0 %copy-start = (f32[32,301]{1,0:T(8,128)S(1)}, f32[32,301]{1,0:T(8,128)}, u32[]{:S(2)}) copy-start(f32[32,301]{1,0:T(8,128)} %get-tuple-element.9) | copy-start | bytes 115588
